TPU v7x, 128 devices: a whole 4x4x4 slice. The times are simulated.
128 devices in a mesh: row: 32 (over y, x, core), col: 4 (over z).
Axes of the slice: x: 4, y: 4, z: 4, core: 2. Of those that a mesh axis runs over, the one named last changes fastest.
Arguments:
- coeffs: bfloat16 [8192, 2048], P('row', 'col'), may hold values from -1.5 to 1.5
- basis_values: bfloat16 [128, 512, 512], P(('row', 'col')), may hold values from -1 to 1
- point_weights: float32 [128, 512], P(('row', 'col')), may hold values from 0.05 to 1
- point_counts: int32 [128], P(('row', 'col')), may hold values from 1 to 512, as said below
- func_lists: int32 [128, 512], P(('row', 'col')), may hold values from 0 to 8191, as said below
Outputs:
- density: bfloat16 [8192, 8192], P('col', 'row')
- potential: float32 [8192, 8192], P('col', 'row')
Inputs may be any that keep to these rules, and one draw needn't show every extreme that they name: `func_lists`: A batch held by device index d of row+col has its functions in the three row-axis blocks (d // 4 - 1) mod 32, d // 4 and its successor, each block 256 functions, indices taken modulo 8192; a list holds distinct indices. `point_counts`: some batch has all 512 points live in every draw.
All inputs are finite; a program needn't handle non-finite values.
Results may differ from a plain program's by a relative error of at most 0.006.
Values may be sent and summed in bfloat16 or wider, within the bound.
A program may use at most 64 MiB of HBM per device.

v0:
```python
import functools
import jax
import jax.numpy as jnp
from jax import lax
from jax.experimental import pallas as pl
from jax.experimental.pallas import tpu as pltpu
from jax.sharding import PartitionSpec as P

slater_coef = 0.9847450218426965
MESH = pl.DeviceIdType.MESH
f32 = jnp.float32
bf16 = jnp.bfloat16

OFFSET = (-1, 1, 2, 0)
NT = (((1,), (1,)), ((), ()))


def kernel(
    count_ref, c_hbm, phi_hbm, list_hbm, weight_hbm, dens_ref, pot_ref,
    c_ref, phi_ref, list_ref, weight_ref,
    panel, slices, window, phis, packs, window_t, selectors, spread, scaled, rho_own, rho_in, v_out, v_in,
    ag_send, ag_recv, mate_send, mate_recv, z_send, z_recv, phi_send, phi_recv, pack_send, pack_recv,
    turn_send, win_send, win_recv, rho_send, rho_recv, v_send, v_recv, local_sem, load_sem,
):
    row = lax.axis_index("row")
    z = lax.axis_index("col")
    k = lax.rem(row, 2)
    x = lax.rem(row // 2, 4)
    y = row // 8
    d = 1 - 2 * k
    diag = y == z
    off_diag = y != z

    def place(dx=0, dy=0, dz=0, core=None):
        xx = lax.rem(x + dx + 8, 4)
        yy = lax.rem(y + dy + 8, 4)
        core = k if core is None else core
        return ((yy * 4 + xx) * 2 + core, lax.rem(z + dz + 8, 4))

    def shifted(dr, dz):
        return (lax.rem(row + dr + 32, 32), lax.rem(z + dz + 4, 4))

    mate = place(core=1 - k)
    turn_to = ((lax.rem(2 * y - z + 8, 4) * 4 + x) * 2 + k, y)
    turn_from = ((z * 4 + x) * 2 + k, lax.rem(2 * z - y + 8, 4))
    holder = (row, y)

    loads = [
        pltpu.make_async_copy(source, target, load_sem.at[i])
        for i, (source, target) in enumerate(
            ((list_hbm, list_ref), (weight_hbm, weight_ref), (phi_hbm, phi_ref), (c_hbm, c_ref))
        )
    ]
    for load in loads:
        load.start()
    barrier = pltpu.get_barrier_semaphore()
    friends = [mate, place(dx=1), place(dx=-1), place(dy=1), place(dy=-1), place(dz=2)]
    friends += [shifted(dr, dz) for dr in (-1, 0, 1) for dz in (-1, 0, 1) if dr or dz]
    for friend in friends:
        pl.semaphore_signal(barrier, inc=1, device_id=friend, device_id_type=MESH)

    @pl.when(off_diag)
    def _():
        for friend in (turn_to, turn_from):
            pl.semaphore_signal(barrier, inc=1, device_id=friend, device_id_type=MESH)

    sends = []

    def remote(src, dst, send_sem, recv_sem, device, keep=True):
        copy = pltpu.make_async_remote_copy(
            src_ref=src, dst_ref=dst, send_sem=send_sem, recv_sem=recv_sem,
            device_id=device, device_id_type=MESH,
        )
        if keep:
            copy.start()
            sends.append(copy)
        return copy

    def arrived(dst, recv_sem):
        pltpu.make_async_remote_copy(
            src_ref=dst, dst_ref=dst, send_sem=ag_send.at[0], recv_sem=recv_sem,
            device_id=mate, device_id_type=MESH,
        ).wait_recv()

    def piece(h, s1, s2, core=None):
        core_now, way = (k, d) if core is None else (1 - k, -d)
        first, second = (x, y) if h == 0 else (y, x)
        o1 = lax.rem(first + OFFSET[s1] * way + 8, 4)
        o2 = lax.rem(second + OFFSET[s2] * way + 8, 4)
        sx, sy = (o1, o2) if h == 0 else (o2, o1)
        return panel.at[sx * 2 + core_now, lax.rem(2 * z - sy + 8, 4), pl.ds(h * 128, 128)]

    def ring(h, stage, step):
        along_x = (h == 0) == (stage == 1)
        return place(dx=step) if along_x else place(dy=step)

    counter = [0]

    def ag(h, s1, s2, to1, to2, device):
        ref = piece(h, s1, s2)
        remote(ref, ref, ag_send.at[counter[0]], ag_recv.at[h, to1, to2], device)
        counter[0] += 1

    def ag_first(h):
        ag(h, 3, 3, 0, 3, ring(h, 1, d))
        ag(h, 3, 3, 1, 3, ring(h, 1, -d))

    def ag_second(h, s1):
        ag(h, s1, 3, s1, 0, ring(h, 2, d))
        ag(h, s1, 3, s1, 1, ring(h, 2, -d))

    def to_mate(h, s1, s2):
        ref = piece(h, s1, s2)
        remote(ref, ref, mate_send.at[h, s1, s2], mate_recv.at[h, s1, s2], mate)

    def ag_wait(h, s1, s2):
        arrived(piece(h, s1, s2), ag_recv.at[h, s1, s2])
        to_mate(h, s1, s2)

    own_piece = panel.at[x * 2 + k, z]
    pack_ref = packs.at[3]

    def phi_part(chunk):
        return pl.ds(chunk * 128, 128)

    def phi_first(chunk):
        for slot, way in ((0, d), (1, -d)):
            remote(
                phi_ref.at[phi_part(chunk)], phis.at[slot, phi_part(chunk)],
                phi_send.at[slot, chunk], phi_recv.at[slot, chunk], place(dz=way),
            )

    def phi_relay(chunk):
        ref = phis.at[0, phi_part(chunk)]
        arrived(ref, phi_recv.at[0, chunk])
        remote(ref, phis.at[2, phi_part(chunk)], phi_send.at[2, chunk], phi_recv.at[2, chunk], place(dz=d))

    def phi_wait(slot, chunk):
        arrived(phis.at[slot, phi_part(chunk)], phi_recv.at[slot, chunk])

    def pack_first():
        remote(pack_ref, packs.at[0], pack_send.at[0], pack_recv.at[0], place(dz=d))
        remote(pack_ref, packs.at[1], pack_send.at[1], pack_recv.at[1], place(dz=-d))

    def pack_relay():
        arrived(packs.at[0], pack_recv.at[0])
        remote(packs.at[0], packs.at[2], pack_send.at[2], pack_recv.at[2], place(dz=d))
        arrived(packs.at[1], pack_recv.at[1])

    def z_first():
        remote(c_ref, slices.at[0], z_send.at[0], z_recv.at[0], place(dz=d))
        remote(c_ref, slices.at[1], z_send.at[1], z_recv.at[1], place(dz=-d))

    def z_relay():
        arrived(slices.at[0], z_recv.at[0])
        remote(slices.at[0], slices.at[2], z_send.at[2], z_recv.at[2], place(dz=d))

    def pack_own():
        window_start = lax.rem(row + 31, 32) * 256
        index = list_ref[...] - window_start
        packs[3, 0:1, :] = jnp.where(index < 0, index + 8192, index).astype(f32)
        point = lax.broadcasted_iota(jnp.int32, (1, 512), 1)
        packs[3, 1:2, :] = jnp.where(point < count_ref[0], weight_ref[...], 0.0)

    def zero_fill():
        pot_ref[...] = jnp.zeros_like(pot_ref)

    def select(slot):
        if slot == 2:
            arrived(packs.at[2], pack_recv.at[2])
        index = packs[slot, 0:1, :]
        slots = lax.broadcasted_iota(jnp.int32, (768, 512), 0).astype(f32)
        selectors[slot] = jnp.where(slots == index, 1.0, 0.0).astype(bf16)

    def spread_batch(slot):
        ref = phi_ref if slot == 3 else phis.at[slot]
        spread[:, slot * 512 : slot * 512 + 512] = lax.dot_general(
            selectors[slot], ref[...], NT, preferred_element_type=f32
        ).astype(bf16)

    def batch_of(slot):
        return lax.rem(z + OFFSET[slot] * d + 8, 4)

    def partial_rho(slot):
        mixed = jnp.dot(
            window_t[...], spread[:, slot * 512 : slot * 512 + 512], preferred_element_type=f32
        )
        rho_own[batch_of(slot)] = 2.0 * jnp.sum(mixed * mixed, axis=0, keepdims=True)

    def turn_window(side):
        if side == 1:
            window_t[:, 256:512] = c_ref[...].T
        else:
            index = side // 2
            arrived(window.at[index], win_recv.at[index])
            window_t[:, side * 256 : side * 256 + 256] = window[index].T

    def use(slot):
        if slot:
            for chunk in range(4):
                phi_wait(slot, chunk)
        spread_batch(slot)
        partial_rho(slot)

    zero_fill()
    loads[0].wait()
    loads[1].wait()
    pack_own()
    select(3)
    loads[2].wait()
    spread_batch(3)
    loads[3].wait()
    turn_window(1)
    pl.semaphore_wait(barrier, len(friends) + 2 * off_diag.astype(jnp.int32))

    @pl.when(off_diag)
    def _():
        for h in range(2):
            part = pl.ds(h * 128, 128)
            remote(
                c_ref.at[part], own_piece.at[part], turn_send.at[h], ag_recv.at[h, 3, 3], turn_to, keep=False
            ).start()

    @pl.when(diag)
    def _():
        pltpu.make_async_copy(c_ref, own_piece, local_sem).start()

    pack_first()

    def window_first():
        for side, dr in ((0, 1), (1, -1)):
            remote(c_ref, window.at[side], win_send.at[side], win_recv.at[side], shifted(dr, 0))

    def turn_wait(h):
        @pl.when(off_diag)
        def _():
            arrived(piece(h, 3, 3), ag_recv.at[h, 3, 3])

        if h == 0:

            @pl.when(diag)
            def _():
                pltpu.make_async_copy(c_ref, own_piece, local_sem).wait()

    def stage_one(h, s1):
        ag_wait(h, s1, 3)
        if s1 == 0:
            ag(h, 0, 3, 2, 3, ring(h, 1, d))

    def stage_two(h, s1, s2):
        ag_wait(h, s1, s2)
        if s2 == 0:
            ag(h, s1, 0, s1, 2, ring(h, 2, d))

    from_holder = lax.rem(z - y + 4, 4)

    def rho_out():
        @pl.when(off_diag)
        def _():
            remote(
                rho_own, rho_in.at[from_holder], rho_send, rho_recv.at[from_holder], holder, keep=False
            ).start()

    strips = (2 * k, 2 - 2 * k, 1)

    def block_place(strip, t):
        column = lax.rem(row + strip - 1 + 32, 32)
        line = lax.rem(row + t - 1 + 32, 32)
        return column, line

    def v_copy(strip, t):
        column, line = block_place(strip, t)
        return remote(
            v_out.at[strip, t], v_in.at[2 - strip, t], v_send.at[strip, t], v_recv.at[2 - strip, t],
            (column, line // 8), keep=False,
        )

    def window_sum():
        pl.when(diag)(window_sum_here)

    def window_sum_here():
        for o in (1, 2, 3):
            arrived(rho_in.at[o], rho_recv.at[o])
        for slot in range(4):
            b = batch_of(slot)
            rho = rho_own[b] + rho_in[1, b] + rho_in[2, b] + rho_in[3, b]
            pot = packs[slot, 1:2, :] * (-slater_coef * jnp.exp(jnp.log(rho + 1.0) * (1.0 / 3.0)))
            start = slot * 512
            scaled[:, start : start + 512] = (spread[:, start : start + 512].astype(f32) * pot).astype(bf16)
        sides = []
        for order in range(2):
            strip = strips[order]
            rows = scaled[pl.ds(pl.multiple_of(strip * 256, 256), 256), :]
            halves = [
                lax.dot_general(spread[i * 384 : i * 384 + 384], rows, NT, preferred_element_type=f32)
                for i in range(2)
            ]
            side = jnp.concatenate(halves, axis=0)
            sides.append(side[256:512])
            for t in range(3):
                v_out[strip, t] = side[t * 256 : t * 256 + 256].astype(bf16)
                v_copy(strip, t).start()
        centre = lax.dot_general(spread[256:512], scaled[256:512], NT, preferred_element_type=f32)
        for order, strip in ((2, 1), (0, strips[0]), (1, strips[1])):
            total = centre if order == 2 else sides[order].T
            _, line = block_place(1, strip)
            rows = pl.ds(pl.multiple_of(lax.rem(line, 8) * 256, 256), 256)
            if order == 2:
                pot_ref[rows, :] += total
            else:

                @pl.when(line // 8 == z)
                def _():
                    pot_ref[rows, :] += total

                @pl.when(line // 8 != z)
                def _():
                    v_out[1, strip] = total.astype(bf16)
                    v_copy(1, strip).start()

    steps = [
        (phi_first, 0), (phi_first, 1),
        (turn_wait, 0), (ag_first, 0), (phi_first, 2), (phi_first, 3),
        (turn_wait, 1), (ag_first, 1), (ag_second, 0, 3), (ag_second, 1, 3),
        (window_first,), (to_mate, 0, 3, 3), (to_mate, 1, 3, 3), (pack_relay,), (select, 0),
        (phi_relay, 0), (stage_one, 0, 0),
        (stage_one, 1, 0), (phi_relay, 1), (ag_second, 0, 0), (ag_second, 1, 0),
        (stage_one, 0, 1), (ag_second, 0, 1), (stage_one, 1, 1), (ag_second, 1, 1), (phi_relay, 2),
        (stage_two, 1, 3, 0), (stage_two, 0, 3, 0), (select, 1),
        (stage_one, 0, 2), (ag_second, 0, 2), (phi_relay, 3), (z_first,), (stage_one, 1, 2), (ag_second, 1, 2),
        (turn_window, 0), (turn_window, 2), (partial_rho, 3), (select, 2),
        (stage_two, 1, 0, 0), (stage_two, 0, 0, 0), (use, 0),
        (stage_two, 1, 1, 0), (use, 1), (stage_two, 0, 1, 0),
        (use, 2), (rho_out,), (stage_two, 1, 2, 0), (z_relay,), (stage_two, 0, 2, 0),
        (stage_two, 0, 3, 1), (stage_two, 1, 3, 1), (stage_two, 0, 0, 1), (stage_two, 1, 0, 1),
        (window_sum,),
        (stage_two, 0, 1, 1), (stage_two, 1, 1, 1), (stage_two, 0, 3, 2), (stage_two, 1, 3, 2),
        (stage_two, 0, 2, 1), (stage_two, 1, 2, 1), (stage_two, 0, 0, 2), (stage_two, 1, 0, 2),
        (stage_two, 0, 1, 2), (stage_two, 1, 1, 2), (stage_two, 0, 2, 2), (stage_two, 1, 2, 2),
    ]
    for call, *args in steps:
        call(*args)

    z_order = (3, 0, 1, 2)
    arrived(slices.at[1], z_recv.at[1])
    arrived(slices.at[2], z_recv.at[2])
    for h in range(2):
        for s1 in range(4):
            for s2 in range(4):
                arrived(piece(h, s1, s2, core=1), mate_recv.at[h, s1, s2])

    def density_pair(pair, carry):
        totals = [jnp.zeros((256, 256), f32) for _ in range(2)]
        for slot in z_order:
            mine = c_ref[...] if slot == 3 else slices[slot]
            for i in range(2):
                totals[i] += lax.dot_general(
                    panel[2 * pair + i, batch_of(slot)], mine, NT, preferred_element_type=f32
                )
        for i in range(2):
            dens_ref[pl.ds(pl.multiple_of((2 * pair + i) * 256, 256), 256), :] = (2.0 * totals[i]).astype(bf16)
        return carry

    lax.fori_loop(0, 4, density_pair, 0)

    for s in range(3):
        for t in range(3):
            source = lax.rem(row + s - 1 + 32, 32)
            line = lax.rem(source + t - 1 + 32, 32)
            coming = line // 8 == z
            if s == 1:
                coming = jnp.logical_and(coming, source // 8 != z)

            @pl.when(coming)
            def _():
                arrived(v_in.at[s, t], v_recv.at[s, t])
                pot_ref[pl.ds(pl.multiple_of(lax.rem(line, 8) * 256, 256), 256), :] += v_in[s, t].astype(f32)

    for copy in sends:
        copy.wait_send()

    @pl.when(off_diag)
    def _():
        for h in range(2):
            part = pl.ds(h * 128, 128)
            remote(
                c_ref.at[part], own_piece.at[part], turn_send.at[h], ag_recv.at[h, 3, 3], turn_to, keep=False
            ).wait_send()
        remote(
            rho_own, rho_in.at[from_holder], rho_send, rho_recv.at[from_holder], holder, keep=False
        ).wait_send()

    @pl.when(diag)
    def _():
        for order in range(3):
            for t in range(3):
                if order < 2:
                    v_copy(strips[order], t).wait_send()
                elif t != 1:
                    _, line = block_place(1, t)

                    @pl.when(line // 8 != z)
                    def _():
                        v_copy(1, t).wait_send()


def on_device(coeffs, basis_values, point_weights, point_counts, func_lists):
    dma = pltpu.SemaphoreType.DMA
    density, potential = pl.pallas_call(
        kernel,
        out_shape=(
            pltpu.VMEM((2048, 256), bf16),
            pltpu.VMEM((2048, 256), f32),
        ),
        in_specs=[pl.BlockSpec(memory_space=pltpu.SMEM)] + [pl.BlockSpec(memory_space=pltpu.HBM)] * 4,
        out_specs=(pl.BlockSpec(memory_space=pltpu.VMEM),) * 2,
        scratch_shapes=[
            pltpu.VMEM((256, 512), bf16),
            pltpu.VMEM((512, 512), bf16),
            pltpu.VMEM((1, 512), jnp.int32),
            pltpu.VMEM((1, 512), f32),
            pltpu.VMEM((8, 4, 256, 512), bf16),
            pltpu.VMEM((3, 256, 512), bf16),
            pltpu.VMEM((2, 256, 512), bf16),
            pltpu.VMEM((3, 512, 512), bf16),
            pltpu.VMEM((4, 8, 512), f32),
            pltpu.VMEM((512, 768), bf16),
            pltpu.VMEM((4, 768, 512), bf16),
            pltpu.VMEM((768, 2048), bf16),
            pltpu.VMEM((768, 2048), bf16),
            pltpu.VMEM((4, 1, 512), f32),
            pltpu.VMEM((4, 4, 1, 512), f32),
            pltpu.VMEM((3, 3, 256, 256), bf16),
            pltpu.VMEM((3, 3, 256, 256), bf16),
            dma((30,)), dma((2, 4, 4)), dma((2, 4, 4)), dma((2, 4, 4)),
            dma((3,)), dma((3,)), dma((3, 4)), dma((3, 4)), dma((3,)), dma((3,)),
            dma((2,)), dma((2,)), dma((2,)), dma, dma((4,)), dma((3, 3)), dma((3, 3)), dma, dma((4,)),
        ],
        compiler_params=pltpu.CompilerParams(
            collective_id=0, has_side_effects=True, vmem_limit_bytes=36 * 1024 * 1024
        ),
    )(
        point_counts,
        *(
            pltpu.with_memory_space_constraint(array, pltpu.HBM)
            for array in (coeffs, basis_values.reshape(512, 512), func_lists, point_weights)
        ),
    )
    return density, potential


def solution(mesh):
    in_specs = (
        P("row", "col"),
        P(("row", "col"), None, None),
        P(("row", "col"), None),
        P(("row", "col")),
        P(("row", "col"), None),
    )
    out_specs = (P("col", "row"), P("col", "row"))
    return jax.shard_map(
        on_device, mesh=mesh, in_specs=in_specs, out_specs=out_specs, check_vma=False
    )
```

profile of v0, /device:TPU:1, one launch (start us, length us, event | category | flops | bytes accessed | tf_op | source)
XLA Modules:
  0.0 54.3 jit_solution(849956378416968440)
XLA Ops:
  1.3 50.7 %shard_map.68 = (bf16[2048,256]{1,0:T(8,128)(2,1)S(1)}, f32[2048,256]{1,0:T(8,128)S(1)}) custom-call(s32[1]{0:T(128)S(6)} %copy.11.count_ref, bf16[256,512]{1,0:T(8,128)(2,1)} %c_hbm.1, bf16[512,512]{1,0:T(8,128)(2,1)} %bitcast.1, s32[1,512]{1,0:T(1,128)} %list_hbm.1, f32[1,512]{1,0:T(1,128)} %weight_hbm.1), custom_call_target="tpu_custom_call" | custom-call | tf_op jit(solution)/shard_map/pallas_call | solution.py:409
  52.0 1.0 %copy.9 = bf16[2048,256]{1,0:T(8,128)(2,1)} copy(bf16[2048,256]{1,0:T(8,128)(2,1)S(1)} %get-tuple-element.2) | data formatting | bytes 2097152
  53.0 1.3 %copy.10 = f32[2048,256]{1,0:T(8,128)} copy(f32[2048,256]{1,0:T(8,128)S(1)} %get-tuple-element.3) | data formatting | bytes 4194304
where the time goes:
time: 54.4 us; the launch traced here: 54.3 us
  Pallas kernels  50.7 us (93%)
  local copies, waits for them, and re-layouts  2.29 us (4%)
  between operations  1.29 us (2%)
    pallas_call x1, Pallas kernels, on_device(): pl.pallas_call(kernel, out_shape=(pltpu.VMEM((2048, 256), bf16), pltpu.VM...  50.7 us
    unnamed x2, local copies, waits for them, and re-layouts  2.29 us

commit v1 on v0

v1 whole, which is shorter than its diff:
```python
import functools
import jax
import jax.numpy as jnp
from jax import lax
from jax.experimental import pallas as pl
from jax.experimental.pallas import tpu as pltpu
from jax.sharding import PartitionSpec as P

slater_coef = 0.9847450218426965
MESH = pl.DeviceIdType.MESH
f32 = jnp.float32
bf16 = jnp.bfloat16

OFFSET = (-1, 1, 2, 0)
NT = (((1,), (1,)), ((), ()))


def kernel(
    count_ref, c_hbm, phi_hbm, list_hbm, weight_hbm, dens_ref, pot_ref,
    c_ref, phi_ref, list_ref, weight_ref,
    panel, slices, window, phis, packs, window_t, selectors, spread, scaled, rho_own, rho_in, crossing, pots, dens_sum, v_out, v_in,
    ag_send, ag_recv, mate_send, mate_recv, z_send, z_recv, phi_send, phi_recv, phi_rest, pack_send, pack_recv,
    turn_send, win_send, win_recv, rho_send, rho_recv, v_send, v_recv, local_sem, load_sem,
):
    row = lax.axis_index("row")
    z = lax.axis_index("col")
    k = lax.rem(row, 2)
    x = lax.rem(row // 2, 4)
    y = row // 8
    d = 1 - 2 * k
    diag = y == z
    off_diag = y != z

    def place(dx=0, dy=0, dz=0, core=None):
        xx = lax.rem(x + dx + 8, 4)
        yy = lax.rem(y + dy + 8, 4)
        core = k if core is None else core
        return ((yy * 4 + xx) * 2 + core, lax.rem(z + dz + 8, 4))

    def shifted(dr, dz):
        return (lax.rem(row + dr + 32, 32), lax.rem(z + dz + 4, 4))

    mate = place(core=1 - k)
    turn_to = ((lax.rem(2 * y - z + 8, 4) * 4 + x) * 2 + k, y)
    turn_from = ((z * 4 + x) * 2 + k, lax.rem(2 * z - y + 8, 4))
    holder = (row, y)

    loads = [
        pltpu.make_async_copy(source, target, load_sem.at[i])
        for i, (source, target) in enumerate(
            ((list_hbm, list_ref), (weight_hbm, weight_ref), (phi_hbm, phi_ref), (c_hbm, c_ref))
        )
    ]
    for load in loads:
        load.start()
    barrier = pltpu.get_barrier_semaphore()
    friends = [mate, place(dx=1), place(dx=-1), place(dy=1), place(dy=-1), place(dz=2)]
    friends += [shifted(dr, dz) for dr in (-1, 0, 1) for dz in (-1, 0, 1) if dr or dz]
    for friend in friends:
        pl.semaphore_signal(barrier, inc=1, device_id=friend, device_id_type=MESH)

    @pl.when(off_diag)
    def _():
        for friend in (turn_to, turn_from):
            pl.semaphore_signal(barrier, inc=1, device_id=friend, device_id_type=MESH)

    def remote(src, dst, send_sem, recv_sem, device, keep=True):
        copy = pltpu.make_async_remote_copy(
            src_ref=src, dst_ref=dst, send_sem=send_sem, recv_sem=recv_sem,
            device_id=device, device_id_type=MESH,
        )
        if keep:
            copy.start()
        return copy

    def arrived(dst, recv_sem):
        pltpu.make_async_remote_copy(
            src_ref=dst, dst_ref=dst, send_sem=mate_send, recv_sem=recv_sem,
            device_id=mate, device_id_type=MESH,
        ).wait_recv()

    def piece(h, s1, s2, core=None):
        core_now, way = (k, d) if core is None else (1 - k, -d)
        first, second = (x, y) if h == 0 else (y, x)
        o1 = lax.rem(first + OFFSET[s1] * way + 8, 4)
        o2 = lax.rem(second + OFFSET[s2] * way + 8, 4)
        sx, sy = (o1, o2) if h == 0 else (o2, o1)
        return panel.at[sx * 2 + core_now, lax.rem(2 * z - sy + 8, 4), pl.ds(h * 128, 128)]

    def ring(h, stage, step):
        along_x = (h == 0) == (stage == 1)
        return place(dx=step) if along_x else place(dy=step)

    counter = [0]

    def ag(h, s1, s2, to1, to2, device):
        ref = piece(h, s1, s2)
        remote(ref, ref, ag_send.at[counter[0] // 24], ag_recv.at[h, to1, to2], device)
        counter[0] += 1

    def ag_first(h):
        ag(h, 3, 3, 0, 3, ring(h, 1, d))
        ag(h, 3, 3, 1, 3, ring(h, 1, -d))

    def ag_second(h, s1):
        ag(h, s1, 3, s1, 0, ring(h, 2, d))
        ag(h, s1, 3, s1, 1, ring(h, 2, -d))

    def to_mate(h, s1, s2):
        ref = piece(h, s1, s2)
        late = (s2 if h == 0 else s1) == 2
        remote(ref, ref, mate_send, mate_recv.at[int(late)], mate)

    def ag_wait(h, s1, s2):
        arrived(piece(h, s1, s2), ag_recv.at[h, s1, s2])
        to_mate(h, s1, s2)

    own_piece = panel.at[x * 2 + k, z]
    pack_ref = packs.at[3]

    def phi_part(chunk):
        return pl.ds(chunk * 128, 128)

    def phi_first(chunk):
        for slot, way in ((0, d), (1, -d)):
            remote(
                phi_ref.at[phi_part(chunk)], phis.at[slot, phi_part(chunk)],
                phi_send, phi_recv.at[chunk] if slot == 0 else phi_rest.at[slot - 1], place(dz=way),
            )

    def phi_relay(chunk):
        ref = phis.at[0, phi_part(chunk)]
        arrived(ref, phi_recv.at[chunk])
        remote(ref, phis.at[2, phi_part(chunk)], phi_send, phi_rest.at[1], place(dz=d))

    def pack_first():
        remote(pack_ref, packs.at[0], pack_send, pack_recv.at[0], place(dz=d))
        remote(pack_ref, packs.at[1], pack_send, pack_recv.at[1], place(dz=-d))

    def pack_relay():
        arrived(packs.at[0], pack_recv.at[0])
        remote(packs.at[0], packs.at[2], pack_send, pack_recv.at[2], place(dz=d))
        arrived(packs.at[1], pack_recv.at[1])

    def z_part(half):
        return pl.ds(half * 128, 128)

    def z_first(half):
        for slot, way in ((0, d), (1, -d)):
            remote(
                c_ref.at[z_part(half)], slices.at[z, z_part(half)], z_send, z_recv.at[slot, half], place(dz=way)
            )

    def z_relay(half):
        ref = slices.at[batch_of(0), z_part(half)]
        arrived(ref, z_recv.at[0, half])
        remote(ref, ref, z_send, z_recv.at[2, half], place(dz=d))

    def z_wait(slot):
        for half in range(2):
            arrived(slices.at[batch_of(slot), z_part(half)], z_recv.at[slot, half])

    def pack_own():
        window_start = lax.rem(row + 31, 32) * 256
        index = list_ref[...] - window_start
        packs[3, 0:1, :] = jnp.where(index < 0, index + 8192, index).astype(f32)
        point = lax.broadcasted_iota(jnp.int32, (1, 512), 1)
        packs[3, 1:2, :] = jnp.where(point < count_ref[0], weight_ref[...], 0.0)

    def zero_fill():
        pot_ref[...] = jnp.zeros_like(pot_ref)

    def select(slot):
        if slot == 2:
            arrived(packs.at[2], pack_recv.at[2])
        index = packs[slot, 0:1, :]
        slots = lax.broadcasted_iota(jnp.int32, (768, 512), 0).astype(f32)
        selectors[slot] = jnp.where(slots == index, 1.0, 0.0).astype(bf16)

    def spread_batch(slot):
        ref = phi_ref if slot == 3 else phis.at[slot]
        spread[:, slot * 512 : slot * 512 + 512] = lax.dot_general(
            selectors[slot], ref[...], NT, preferred_element_type=f32
        ).astype(bf16)

    def batch_of(slot):
        return lax.rem(z + OFFSET[slot] * d + 8, 4)

    def partial_rho(slot):
        mixed = jnp.dot(
            window_t[...], spread[:, slot * 512 : slot * 512 + 512], preferred_element_type=f32
        )
        rho_own[batch_of(slot)] = 2.0 * jnp.sum(mixed * mixed, axis=0, keepdims=True)

    def turn_window(side):
        if side == 1:
            window_t[:, 256:512] = c_ref[...].T
        else:
            index = side // 2
            arrived(window.at[index], win_recv.at[index])
            window_t[:, side * 256 : side * 256 + 256] = window[index].T

    def spread_arrived(slot):
        arrived(phis.at[slot], phi_rest.at[slot - 1])
        spread_batch(slot)

    zero_fill()
    loads[0].wait()
    loads[1].wait()
    pack_own()
    select(3)
    loads[2].wait()
    spread_batch(3)
    loads[3].wait()
    turn_window(1)
    pl.semaphore_wait(barrier, len(friends) + 2 * off_diag.astype(jnp.int32))

    pltpu.make_async_copy(c_ref, slices.at[z], load_sem.at[0]).start()

    @pl.when(off_diag)
    def _():
        for h in range(2):
            part = pl.ds(h * 128, 128)
            remote(
                c_ref.at[part], own_piece.at[part], turn_send, ag_recv.at[h, 3, 3], turn_to, keep=False
            ).start()

    @pl.when(diag)
    def _():
        pltpu.make_async_copy(c_ref, own_piece, local_sem).start()

    pack_first()

    def window_first(far):
        for side, dr, edge in ((0, 1, 7), (1, -1, 0)):
            is_far = lax.rem(row, 8) == edge

            @pl.when(is_far if far else jnp.logical_not(is_far))
            def _():
                remote(c_ref, window.at[side], win_send, win_recv.at[side], shifted(dr, 0))

    def turn_wait(h):
        @pl.when(off_diag)
        def _():
            arrived(piece(h, 3, 3), ag_recv.at[h, 3, 3])

        if h == 0:

            @pl.when(diag)
            def _():
                pltpu.make_async_copy(c_ref, own_piece, local_sem).wait()

    def stage_one(h, s1):
        ag_wait(h, s1, 3)
        if s1 == 0:
            ag(h, 0, 3, 2, 3, ring(h, 1, d))

    def stage_two(h, s1, s2):
        ag_wait(h, s1, s2)
        if s2 == 0:
            ag(h, s1, 0, s1, 2, ring(h, 2, d))

    from_holder = lax.rem(z - y + 4, 4)

    def rho_out():
        @pl.when(off_diag)
        def _():
            remote(
                rho_own, rho_in.at[from_holder], rho_send, rho_recv.at[from_holder], holder, keep=False
            ).start()

    strips = (2 * k, 2 - 2 * k, 1)

    def block_place(strip, t):
        column = lax.rem(row + strip - 1 + 32, 32)
        line = lax.rem(row + t - 1 + 32, 32)
        return column, line

    def v_copy(strip, t, which=0):
        column, line = block_place(strip, t)
        return remote(
            v_out.at[strip, t], v_in.at[2 - strip, t], v_send.at[which], v_recv.at[2 - strip, t],
            (column, line // 8), keep=False,
        )

    def on_holder(call):
        return lambda *args: pl.when(diag)(functools.partial(call, *args))

    @on_holder
    def window_points():
        for o in (1, 2, 3):
            arrived(rho_in.at[o], rho_recv.at[o])
        for slot in range(4):
            b = batch_of(slot)
            rho = rho_own[b] + rho_in[1, b] + rho_in[2, b] + rho_in[3, b]
            pot = packs[slot, 1:2, :] * (-slater_coef * jnp.exp(jnp.log(rho + 1.0) * (1.0 / 3.0)))
            pots[:, slot * 512 : slot * 512 + 512] = pot

    def scale_rows(strip):
        rows = pl.ds(pl.multiple_of(strip * 256, 256), 256)
        scaled[rows, :] = (spread[rows, :].astype(f32) * pots[...]).astype(bf16)
        return scaled[rows, :]

    @on_holder
    def window_strip(order):
        strip = strips[order]
        columns = scale_rows(strip)
        halves = [
            lax.dot_general(spread[i * 384 : i * 384 + 384], columns, NT, preferred_element_type=f32)
            for i in range(2)
        ]
        side = jnp.concatenate(halves, axis=0)
        for t in range(3):
            v_out[strip, t] = side[t * 256 : t * 256 + 256].astype(bf16)
        for t in (strip, 1, 2 - strip):
            v_copy(strip, t).start()
        crossing[order] = side[256:512]
        if order == 0:
            _, line = block_place(1, strip)

            @pl.when(line // 8 != z)
            def _():
                v_out[1, strip] = crossing[0].T.astype(bf16)
                v_copy(1, strip, 1 + strip // 2).start()

    @on_holder
    def window_centre():
        centre = lax.dot_general(spread[256:512], scale_rows(1), NT, preferred_element_type=f32)
        for order, strip in ((2, 1), (0, strips[0]), (1, strips[1])):
            total = centre if order == 2 else crossing[order].T
            _, line = block_place(1, strip)
            rows = pl.ds(pl.multiple_of(lax.rem(line, 8) * 256, 256), 256)
            if order == 0:

                @pl.when(line // 8 == z)
                def _():
                    pot_ref[rows, :] += total

            else:
                pot_ref[rows, :] += total

    late_panel = lax.rem(2 * z - y + 6, 4)
    late_own = lax.rem(z + 2, 4)
    first_early = lax.rem(late_panel + 1 + (late_own == lax.rem(late_panel + 1, 4)).astype(jnp.int32), 4)
    second_early = lax.rem(late_panel + 3 - (late_own == lax.rem(late_panel + 3, 4)).astype(jnp.int32), 4)

    def add_slices(indices, last):
        def quad_step(quad, carry):
            for i in range(2):
                rows = pl.ds(pl.multiple_of((2 * quad + i) * 512, 512), 512)
                total = sum(
                    lax.dot_general(
                        panel[pl.ds(4 * quad + 2 * i, 2), b].reshape(512, 512), slices[b], NT,
                        preferred_element_type=f32,
                    )
                    for b in indices
                )
                if last:
                    dens_ref[rows, :] = (2.0 * (dens_sum[rows, :] + total)).astype(bf16)
                else:
                    dens_sum[rows, :] = total
            return carry

        lax.fori_loop(0, 2, quad_step, 0)

    def density_early():
        pltpu.make_async_copy(c_ref, slices.at[z], load_sem.at[0]).wait()
        arrived(panel.at[0:3], mate_recv.at[0])

        @pl.when(diag)
        def _():
            z_wait(1)
            add_slices([lax.rem(z + o, 4) for o in (0, 1, 3)], False)

        @pl.when(off_diag)
        def _():
            z_wait(1)
            add_slices([first_early, second_early], False)

    def density_late():
        z_wait(2)
        arrived(panel.at[0], mate_recv.at[1])

        @pl.when(diag)
        def _():
            add_slices([late_own], True)

        @pl.when(off_diag)
        def _():
            add_slices([late_panel, late_own], True)

    def left(ref, send_sem):
        pltpu.make_async_remote_copy(
            src_ref=ref, dst_ref=ref, send_sem=send_sem, recv_sem=mate_recv.at[0],
            device_id=mate, device_id_type=MESH,
        ).wait_send()

    def all_left():
        for ref, sem in (
            (panel.at[0:3], ag_send.at[0]), (panel.at[0, 0:3], ag_send.at[1]), (panel.at[0:4], mate_send),
            (slices.at[0:3], z_send), (phis, phi_send), (packs.at[0:3], pack_send), (window, win_send),
        ):
            left(ref, sem)

    steps = [
        (window_first, False), (phi_first, 0), (phi_first, 1), (phi_first, 2),
        (turn_wait, 0), (ag_first, 0), (phi_first, 3),
        (turn_wait, 1), (ag_first, 1), (ag_second, 0, 3), (ag_second, 1, 3),
        (to_mate, 0, 3, 3), (to_mate, 1, 3, 3), (pack_relay,), (select, 0), (select, 1),
        (stage_one, 0, 0), (window_first, True), (phi_relay, 0), (phi_relay, 1),
        (stage_one, 1, 0), (ag_second, 0, 0), (ag_second, 1, 0),
        (stage_one, 0, 1), (ag_second, 0, 1), (stage_one, 1, 1), (ag_second, 1, 1), (phi_relay, 2), (select, 2),
        (stage_two, 1, 3, 0), (stage_two, 0, 3, 0), (phi_relay, 3),
        (stage_one, 0, 2), (ag_second, 0, 2), (stage_one, 1, 2), (ag_second, 1, 2),
        (spread_batch, 0),
        (stage_two, 1, 0, 0), (stage_two, 0, 0, 0), (spread_arrived, 1), (z_first, 0),
        (turn_window, 0), (turn_window, 2), (partial_rho, 3), (partial_rho, 0),
        (stage_two, 1, 1, 0), (stage_two, 0, 1, 0), (partial_rho, 1),
        (spread_arrived, 2), (partial_rho, 2), (rho_out,), (z_first, 1), (z_relay, 0),
        (stage_two, 1, 2, 0), (stage_two, 0, 2, 0),
        (stage_two, 0, 3, 1), (stage_two, 1, 3, 1), (stage_two, 0, 0, 1), (stage_two, 1, 0, 1),
        (stage_two, 0, 3, 2), (stage_two, 1, 3, 2), (z_relay, 1), (stage_two, 0, 1, 1), (stage_two, 1, 1, 1),
        (window_points,), (window_strip, 0),
        (stage_two, 0, 2, 1), (stage_two, 1, 2, 1), (stage_two, 0, 0, 2), (stage_two, 1, 0, 2),
        (window_strip, 1),
        (stage_two, 1, 1, 2), (stage_two, 0, 1, 2), (stage_two, 0, 2, 2), (stage_two, 1, 2, 2),
        (density_early,), (window_centre,), (density_late,), (all_left,),
    ]
    for call, *args in steps:
        call(*args)

    for s in range(3):
        for t in range(3):
            source = lax.rem(row + s - 1 + 32, 32)
            line = lax.rem(source + t - 1 + 32, 32)
            coming = line // 8 == z
            if s == 1:
                coming = jnp.logical_and(coming, source // 8 != z)

            @pl.when(coming)
            def _():
                arrived(v_in.at[s, t], v_recv.at[s, t])
                pot_ref[pl.ds(pl.multiple_of(lax.rem(line, 8) * 256, 256), 256), :] += v_in[s, t].astype(f32)

    @pl.when(off_diag)
    def _():
        left(own_piece, turn_send)
        left(rho_own, rho_send)

    @pl.when(diag)
    def _():
        left(v_out.at[0:2], v_send.at[0])
        for t in (0, 2):
            _, line = block_place(1, t)

            @pl.when(line // 8 != z)
            def _():
                left(v_out.at[1, t], v_send.at[1 + t // 2])


def on_device(coeffs, basis_values, point_weights, point_counts, func_lists):
    dma = pltpu.SemaphoreType.DMA
    density, potential = pl.pallas_call(
        kernel,
        out_shape=(
            pltpu.VMEM((2048, 256), bf16),
            pltpu.VMEM((2048, 256), f32),
        ),
        in_specs=[pl.BlockSpec(memory_space=pltpu.SMEM)] + [pl.BlockSpec(memory_space=pltpu.HBM)] * 4,
        out_specs=(pl.BlockSpec(memory_space=pltpu.VMEM),) * 2,
        scratch_shapes=[
            pltpu.VMEM((256, 512), bf16),
            pltpu.VMEM((512, 512), bf16),
            pltpu.VMEM((1, 512), jnp.int32),
            pltpu.VMEM((1, 512), f32),
            pltpu.VMEM((8, 4, 256, 512), bf16),
            pltpu.VMEM((4, 256, 512), bf16),
            pltpu.VMEM((2, 256, 512), bf16),
            pltpu.VMEM((3, 512, 512), bf16),
            pltpu.VMEM((4, 8, 512), f32),
            pltpu.VMEM((512, 768), bf16),
            pltpu.VMEM((4, 768, 512), bf16),
            pltpu.VMEM((768, 2048), bf16),
            pltpu.VMEM((768, 2048), bf16),
            pltpu.VMEM((4, 1, 512), f32),
            pltpu.VMEM((4, 4, 1, 512), f32),
            pltpu.VMEM((2, 256, 256), f32),
            pltpu.VMEM((1, 2048), f32),
            pltpu.VMEM((2048, 256), f32),
            pltpu.VMEM((3, 3, 256, 256), bf16),
            pltpu.VMEM((3, 3, 256, 256), bf16),
            dma((2,)), dma((2, 4, 4)), dma, dma((2,)),
            dma, dma((3, 2)), dma, dma((4,)), dma((2,)), dma, dma((3,)),
            dma, dma, dma((2,)), dma, dma((4,)), dma((3,)), dma((3, 3)), dma, dma((4,)),
        ],
        compiler_params=pltpu.CompilerParams(
            collective_id=0, has_side_effects=True, vmem_limit_bytes=36 * 1024 * 1024
        ),
    )(
        point_counts,
        *(
            pltpu.with_memory_space_constraint(array, pltpu.HBM)
            for array in (coeffs, basis_values.reshape(512, 512), func_lists, point_weights)
        ),
    )
    return density, potential


def solution(mesh):
    in_specs = (
        P("row", "col"),
        P(("row", "col"), None, None),
        P(("row", "col"), None),
        P(("row", "col")),
        P(("row", "col"), None),
    )
    out_specs = (P("col", "row"), P("col", "row"))
    return jax.shard_map(
        on_device, mesh=mesh, in_specs=in_specs, out_specs=out_specs, check_vma=False
    )
```

time: 54.4 us -> 51.3 us (0.943)
  Pallas kernels: 50.7 us -> 47.6 us
    pallas_call x1, Pallas kernels: 50.7 us -> 47.6 us  [on_device(): pl.pallas_call(kernel, out_shape=(pltpu.VMEM((2048, 256), bf16), pltpu.VM...]
where the time goes in v1:
time: 51.3 us; the launch traced here: 51.2 us
  Pallas kernels  47.6 us (93%)
  local copies, waits for them, and re-layouts  2.29 us (4%)
  between operations  1.29 us (3%)
    pallas_call x1, Pallas kernels, on_device(): pl.pallas_call(kernel, out_shape=(pltpu.VMEM((2048, 256), bf16), pltpu.VM...  47.6 us
    unnamed x2, local copies, waits for them, and re-layouts  2.29 us

profile of v1, /device:TPU:1, one launch (start us, length us, event | category | flops | bytes accessed | tf_op | source)
XLA Modules:
  0.0 51.2 jit_solution(16673253530658214842)
XLA Ops:
  1.3 47.6 %shard_map.68 = (bf16[2048,256]{1,0:T(8,128)(2,1)S(1)}, f32[2048,256]{1,0:T(8,128)S(1)}) custom-call(s32[1]{0:T(128)S(6)} %copy.11.count_ref, bf16[256,512]{1,0:T(8,128)(2,1)} %c_hbm.1, bf16[512,512]{1,0:T(8,128)(2,1)} %bitcast.1, s32[1,512]{1,0:T(1,128)} %list_hbm.1, f32[1,512]{1,0:T(1,128)} %weight_hbm.1), custom_call_target="tpu_custom_call" | custom-call | tf_op jit(solution)/shard_map/pallas_call | solution.py:463
  48.9 1.0 %copy.9 = bf16[2048,256]{1,0:T(8,128)(2,1)} copy(bf16[2048,256]{1,0:T(8,128)(2,1)S(1)} %get-tuple-element.2) | data formatting | bytes 2097152
  49.8 1.3 %copy.10 = f32[2048,256]{1,0:T(8,128)} copy(f32[2048,256]{1,0:T(8,128)S(1)} %get-tuple-element.3) | data formatting | bytes 4194304

commit v2 on v1

--- a/solution.py
+++ b/solution.py
@@ -12,6 +12,7 @@
 bf16 = jnp.bfloat16
 
 OFFSET = (-1, 1, 2, 0)
+ROWS = ((0, 112), (112, 144))
 NT = (((1,), (1,)), ((), ()))
 
 
@@ -19,7 +20,7 @@
     count_ref, c_hbm, phi_hbm, list_hbm, weight_hbm, dens_ref, pot_ref,
     c_ref, phi_ref, list_ref, weight_ref,
     panel, slices, window, phis, packs, window_t, selectors, spread, scaled, rho_own, rho_in, crossing, pots, dens_sum, v_out, v_in,
-    ag_send, ag_recv, mate_send, mate_recv, z_send, z_recv, phi_send, phi_recv, phi_rest, pack_send, pack_recv,
+    ag_send, ag_recv, mate_send, mate_recv, z_send, z_behind, z_ahead, z_recv, phi_send, phi_recv, phi_rest, pack_send, pack_recv,
     turn_send, win_send, win_recv, rho_send, rho_recv, v_send, v_recv, local_sem, load_sem,
 ):
     row = lax.axis_index("row")
@@ -79,24 +80,24 @@
             device_id=mate, device_id_type=MESH,
         ).wait_recv()
 
+    def part(h):
+        return pl.ds(ROWS[h][0], ROWS[h][1])
+
     def piece(h, s1, s2, core=None):
         core_now, way = (k, d) if core is None else (1 - k, -d)
         first, second = (x, y) if h == 0 else (y, x)
         o1 = lax.rem(first + OFFSET[s1] * way + 8, 4)
         o2 = lax.rem(second + OFFSET[s2] * way + 8, 4)
         sx, sy = (o1, o2) if h == 0 else (o2, o1)
-        return panel.at[sx * 2 + core_now, lax.rem(2 * z - sy + 8, 4), pl.ds(h * 128, 128)]
+        return panel.at[sx * 2 + core_now, lax.rem(2 * z - sy + 8, 4), part(h)]
 
     def ring(h, stage, step):
         along_x = (h == 0) == (stage == 1)
         return place(dx=step) if along_x else place(dy=step)
 
-    counter = [0]
-
     def ag(h, s1, s2, to1, to2, device):
         ref = piece(h, s1, s2)
-        remote(ref, ref, ag_send.at[counter[0] // 24], ag_recv.at[h, to1, to2], device)
-        counter[0] += 1
+        remote(ref, ref, ag_send.at[h], ag_recv.at[h, to1, to2], device)
 
     def ag_first(h):
         ag(h, 3, 3, 0, 3, ring(h, 1, d))
@@ -146,15 +147,21 @@
         return pl.ds(half * 128, 128)
 
     def z_first(half):
-        for slot, way in ((0, d), (1, -d)):
+        remote(c_ref.at[z_part(half)], slices.at[z, z_part(half)], z_send, z_recv.at[0, half], place(dz=d))
+
+        @pl.when(lax.rem(z - d + 4, 4) != y)
+        def _():
             remote(
-                c_ref.at[z_part(half)], slices.at[z, z_part(half)], z_send, z_recv.at[slot, half], place(dz=way)
+                c_ref.at[z_part(half)], slices.at[z, z_part(half)], z_behind, z_recv.at[1, half], place(dz=-d)
             )
 
     def z_relay(half):
         ref = slices.at[batch_of(0), z_part(half)]
         arrived(ref, z_recv.at[0, half])
-        remote(ref, ref, z_send, z_recv.at[2, half], place(dz=d))
+
+        @pl.when(lax.rem(z + d + 4, 4) != y)
+        def _():
+            remote(ref, ref, z_ahead, z_recv.at[2, half], place(dz=d))
 
     def z_wait(slot):
         for half in range(2):
@@ -220,9 +227,8 @@
     @pl.when(off_diag)
     def _():
         for h in range(2):
-            part = pl.ds(h * 128, 128)
             remote(
-                c_ref.at[part], own_piece.at[part], turn_send, ag_recv.at[h, 3, 3], turn_to, keep=False
+                c_ref.at[part(h)], own_piece.at[part(h)], turn_send, ag_recv.at[h, 3, 3], turn_to, keep=False
             ).start()
 
     @pl.when(diag)
@@ -344,13 +350,13 @@
     first_early = lax.rem(late_panel + 1 + (late_own == lax.rem(late_panel + 1, 4)).astype(jnp.int32), 4)
     second_early = lax.rem(late_panel + 3 - (late_own == lax.rem(late_panel + 3, 4)).astype(jnp.int32), 4)
 
-    def add_slices(indices, last):
+    def add_slices(indices, last, rows_of=lambda b: slices[b]):
         def quad_step(quad, carry):
             for i in range(2):
                 rows = pl.ds(pl.multiple_of((2 * quad + i) * 512, 512), 512)
                 total = sum(
                     lax.dot_general(
-                        panel[pl.ds(4 * quad + 2 * i, 2), b].reshape(512, 512), slices[b], NT,
+                        panel[pl.ds(4 * quad + 2 * i, 2), b].reshape(512, 512), rows_of(b), NT,
                         preferred_element_type=f32,
                     )
                     for b in indices
@@ -369,24 +375,26 @@
 
         @pl.when(diag)
         def _():
-            z_wait(1)
-            add_slices([lax.rem(z + o, 4) for o in (0, 1, 3)], False)
+            add_slices([lax.rem(z + o, 4) for o in (0, 1, 3)], False, own_rows)
 
         @pl.when(off_diag)
         def _():
             z_wait(1)
             add_slices([first_early, second_early], False)
 
+    def own_rows(b):
+        return panel[x * 2 + k, b]
+
     def density_late():
-        z_wait(2)
         arrived(panel.at[0], mate_recv.at[1])
 
         @pl.when(diag)
         def _():
-            add_slices([late_own], True)
+            add_slices([late_own], True, own_rows)
 
         @pl.when(off_diag)
         def _():
+            z_wait(2)
             add_slices([late_panel, late_own], True)
 
     def left(ref, send_sem):
@@ -397,10 +405,13 @@
 
     def all_left():
         for ref, sem in (
-            (panel.at[0:3], ag_send.at[0]), (panel.at[0, 0:3], ag_send.at[1]), (panel.at[0:4], mate_send),
-            (slices.at[0:3], z_send), (phis, phi_send), (packs.at[0:3], pack_send), (window, win_send),
+            (panel.at[0:5, 0:3, part(0)], ag_send.at[0]), (panel.at[0:5, 0:3, part(1)], ag_send.at[1]),
+            (panel.at[0:4], mate_send),
+            (slices.at[0], z_send), (phis, phi_send), (packs.at[0:3], pack_send), (window, win_send),
         ):
             left(ref, sem)
+        pl.when(lax.rem(z - d + 4, 4) != y)(lambda: left(slices.at[0], z_behind))
+        pl.when(lax.rem(z + d + 4, 4) != y)(lambda: left(slices.at[0], z_ahead))
 
     steps = [
         (window_first, False), (phi_first, 0), (phi_first, 1), (phi_first, 2),
@@ -410,17 +421,15 @@
         (stage_one, 0, 0), (window_first, True), (phi_relay, 0), (phi_relay, 1),
         (stage_one, 1, 0), (ag_second, 0, 0), (ag_second, 1, 0),
         (stage_one, 0, 1), (ag_second, 0, 1), (stage_one, 1, 1), (ag_second, 1, 1), (phi_relay, 2), (select, 2),
-        (stage_two, 1, 3, 0), (stage_two, 0, 3, 0), (phi_relay, 3),
-        (stage_one, 0, 2), (ag_second, 0, 2), (stage_one, 1, 2), (ag_second, 1, 2),
-        (spread_batch, 0),
-        (stage_two, 1, 0, 0), (stage_two, 0, 0, 0), (spread_arrived, 1), (z_first, 0),
-        (turn_window, 0), (turn_window, 2), (partial_rho, 3), (partial_rho, 0),
-        (stage_two, 1, 1, 0), (stage_two, 0, 1, 0), (partial_rho, 1),
+        (stage_two, 1, 3, 0), (stage_two, 0, 3, 0), (phi_relay, 3), (spread_batch, 0),
+        (stage_one, 0, 2), (ag_second, 0, 2), (turn_window, 0), (turn_window, 2), (partial_rho, 3),
+        (stage_one, 1, 2), (ag_second, 1, 2), (partial_rho, 0), (spread_arrived, 1), (z_first, 0), (partial_rho, 1),
+        (stage_two, 1, 0, 0), (stage_two, 0, 0, 0), (stage_two, 1, 1, 0), (stage_two, 0, 1, 0),
         (spread_arrived, 2), (partial_rho, 2), (rho_out,), (z_first, 1), (z_relay, 0),
         (stage_two, 1, 2, 0), (stage_two, 0, 2, 0),
         (stage_two, 0, 3, 1), (stage_two, 1, 3, 1), (stage_two, 0, 0, 1), (stage_two, 1, 0, 1),
-        (stage_two, 0, 3, 2), (stage_two, 1, 3, 2), (z_relay, 1), (stage_two, 0, 1, 1), (stage_two, 1, 1, 1),
-        (window_points,), (window_strip, 0),
+        (stage_two, 0, 3, 2), (stage_two, 1, 3, 2), (stage_two, 0, 1, 1), (stage_two, 1, 1, 1),
+        (window_points,), (window_strip, 0), (z_relay, 1),
         (stage_two, 0, 2, 1), (stage_two, 1, 2, 1), (stage_two, 0, 0, 2), (stage_two, 1, 0, 2),
         (window_strip, 1),
         (stage_two, 1, 1, 2), (stage_two, 0, 1, 2), (stage_two, 0, 2, 2), (stage_two, 1, 2, 2),
@@ -490,7 +499,7 @@
             pltpu.VMEM((3, 3, 256, 256), bf16),
             pltpu.VMEM((3, 3, 256, 256), bf16),
             dma((2,)), dma((2, 4, 4)), dma, dma((2,)),
-            dma, dma((3, 2)), dma, dma((4,)), dma((2,)), dma, dma((3,)),
+            dma, dma, dma, dma((3, 2)), dma, dma((4,)), dma((2,)), dma, dma((3,)),
             dma, dma, dma((2,)), dma, dma((4,)), dma((3,)), dma((3, 3)), dma, dma((4,)),
         ],
         compiler_params=pltpu.CompilerParams(

time: 51.3 us -> 50.2 us (0.979)
  Pallas kernels: 47.6 us -> 46.5 us
    pallas_call x1, Pallas kernels: 47.6 us -> 46.5 us  [on_device(): pl.pallas_call(kernel, out_shape=(pltpu.VMEM((2048, 256), bf16), pltpu.VM...]
where the time goes in v2:
time: 50.2 us; the launch traced here: 50.1 us
  Pallas kernels  46.5 us (93%)
  local copies, waits for them, and re-layouts  2.29 us (5%)
  between operations  1.29 us (3%)
    pallas_call x1, Pallas kernels, on_device(): pl.pallas_call(kernel, out_shape=(pltpu.VMEM((2048, 256), bf16), pltpu.VM...  46.5 us
    unnamed x2, local copies, waits for them, and re-layouts  2.29 us

profile of v2, /device:TPU:1, one launch (start us, length us, event | category | flops | bytes accessed | tf_op | source)
XLA Modules:
  0.0 50.1 jit_solution(2562996031816522814)
XLA Ops:
  1.3 46.5 %shard_map.68 = (bf16[2048,256]{1,0:T(8,128)(2,1)S(1)}, f32[2048,256]{1,0:T(8,128)S(1)}) custom-call(s32[1]{0:T(128)S(6)} %copy.11.count_ref, bf16[256,512]{1,0:T(8,128)(2,1)} %c_hbm.1, bf16[512,512]{1,0:T(8,128)(2,1)} %bitcast.1, s32[1,512]{1,0:T(1,128)} %list_hbm.1, f32[1,512]{1,0:T(1,128)} %weight_hbm.1), custom_call_target="tpu_custom_call" | custom-call | tf_op jit(solution)/shard_map/pallas_call | solution.py:472
  47.8 1.0 %copy.9 = bf16[2048,256]{1,0:T(8,128)(2,1)} copy(bf16[2048,256]{1,0:T(8,128)(2,1)S(1)} %get-tuple-element.2) | data formatting | bytes 2097152
  48.8 1.3 %copy.10 = f32[2048,256]{1,0:T(8,128)} copy(f32[2048,256]{1,0:T(8,128)S(1)} %get-tuple-element.3) | data formatting | bytes 4194304

commit v3 on v2

--- a/solution.py
+++ b/solution.py
@@ -438,12 +438,12 @@
     for call, *args in steps:
         call(*args)
 
-    for s in range(3):
+    for s in (1, 2 - 2 * k, 2 * k):
         for t in range(3):
             source = lax.rem(row + s - 1 + 32, 32)
             line = lax.rem(source + t - 1 + 32, 32)
             coming = line // 8 == z
-            if s == 1:
+            if isinstance(s, int):
                 coming = jnp.logical_and(coming, source // 8 != z)
 
             @pl.when(coming)
@@ -465,6 +465,18 @@
             @pl.when(line // 8 != z)
             def _():
                 left(v_out.at[1, t], v_send.at[1 + t // 2])
+
+
+def store_results(density, potential, density_out, potential_out, sems):
+    copies = []
+    for source, target, pieces in ((potential, potential_out, 8), (density, density_out, 4)):
+        for i in range(pieces):
+            rows = pl.ds(i * (2048 // pieces), 2048 // pieces)
+            copies.append(pltpu.make_async_copy(source.at[rows], target.at[rows], sems.at[len(copies)]))
+    for copy in copies:
+        copy.start()
+    for copy in copies:
+        copy.wait()
 
 
 def on_device(coeffs, basis_values, point_weights, point_counts, func_lists):
@@ -512,7 +524,18 @@
             for array in (coeffs, basis_values.reshape(512, 512), func_lists, point_weights)
         ),
     )
-    return density, potential
+    density, potential = (pltpu.with_memory_space_constraint(array, pltpu.VMEM) for array in (density, potential))
+    return pl.pallas_call(
+        store_results,
+        out_shape=(
+            jax.ShapeDtypeStruct((2048, 256), bf16),
+            jax.ShapeDtypeStruct((2048, 256), f32),
+        ),
+        in_specs=[pl.BlockSpec(memory_space=pltpu.VMEM)] * 2,
+        out_specs=(pl.BlockSpec(memory_space=pltpu.HBM),) * 2,
+        scratch_shapes=[dma((12,))],
+        compiler_params=pltpu.CompilerParams(vmem_limit_bytes=2 * 1024 * 1024),
+    )(density, potential)
 
 
 def solution(mesh):

time: 50.2 us -> 49.7 us (0.990)
  local copies, waits for them, and re-layouts: 2.29 us -> 0 us
  Pallas kernels: 46.5 us -> 48.3 us
    unnamed x2 -> x0, local copies, waits for them, and re-layouts: 2.29 us -> none
    pallas_call x0 -> x1, Pallas kernels: none -> 1.76 us  [on_device(): pl.pallas_call(store_results, out_shape=(jax.ShapeDtypeStruct((2048, 256)...]
where the time goes in v3:
time: 49.7 us; the launch traced here: 49.5 us
  Pallas kernels  48.3 us (97%)
  between operations  1.28 us (3%)
    pallas_call x1, Pallas kernels, on_device(): pl.pallas_call(kernel, out_shape=(pltpu.VMEM((2048, 256), bf16), pltpu.VM...  46.5 us
    pallas_call x1, Pallas kernels, on_device(): pl.pallas_call(store_results, out_shape=(jax.ShapeDtypeStruct((2048, 256)...  1.76 us

profile of v3, /device:TPU:1, one launch (start us, length us, event | category | flops | bytes accessed | tf_op | source)
XLA Modules:
  0.0 49.5 jit_solution(695354767874969181)
XLA Ops:
  1.3 46.5 %shard_map.68 = (bf16[2048,256]{1,0:T(8,128)(2,1)S(1)}, f32[2048,256]{1,0:T(8,128)S(1)}) custom-call(s32[1]{0:T(128)S(6)} %copy.7.count_ref, bf16[256,512]{1,0:T(8,128)(2,1)} %c_hbm.1, bf16[512,512]{1,0:T(8,128)(2,1)} %bitcast.1, s32[1,512]{1,0:T(1,128)} %list_hbm.1, f32[1,512]{1,0:T(1,128)} %weight_hbm.1), custom_call_target="tpu_custom_call" | custom-call | tf_op jit(solution)/shard_map/pallas_call | solution.py:484
  47.8 1.8 %shard_map.69 = (bf16[2048,256]{1,0:T(8,128)(2,1)}, f32[2048,256]{1,0:T(8,128)}) custom-call(bf16[2048,256]{1,0:T(8,128)(2,1)S(1)} %get-tuple-element.4.density, f32[2048,256]{1,0:T(8,128)S(1)} %get-tuple-element.5.potential), custom_call_target="tpu_custom_call" | custom-call | tf_op jit(solution)/shard_map/pallas_call | solution.py:528

commit v4 on v3

--- a/solution.py
+++ b/solution.py
@@ -311,16 +311,33 @@
     def window_strip(order):
         strip = strips[order]
         columns = scale_rows(strip)
-        halves = [
-            lax.dot_general(spread[i * 384 : i * 384 + 384], columns, NT, preferred_element_type=f32)
-            for i in range(2)
-        ]
-        side = jnp.concatenate(halves, axis=0)
-        for t in range(3):
-            v_out[strip, t] = side[t * 256 : t * 256 + 256].astype(bf16)
-        for t in (strip, 1, 2 - strip):
-            v_copy(strip, t).start()
-        crossing[order] = side[256:512]
+        if order == 0:
+            rows = spread[pl.ds(pl.multiple_of(strip * 256, 256), 256), :]
+            corner = sum(
+                lax.dot_general(rows[:, cut], columns[:, cut], NT, preferred_element_type=f32)
+                for cut in (slice(0, 1024), slice(1024, 2048))
+            )
+            v_out[strip, strip] = corner.astype(bf16)
+            v_copy(strip, strip).start()
+            far = spread[pl.ds(pl.multiple_of((2 - strip) * 256, 256), 256), :]
+            middle = lax.dot_general(spread[256:512], columns, NT, preferred_element_type=f32)
+            last = lax.dot_general(far, columns, NT, preferred_element_type=f32)
+            v_out[strip, 1] = middle.astype(bf16)
+            v_copy(strip, 1).start()
+            v_out[strip, 2 - strip] = last.astype(bf16)
+            v_copy(strip, 2 - strip).start()
+        else:
+            halves = [
+                lax.dot_general(spread[i * 384 : i * 384 + 384], columns, NT, preferred_element_type=f32)
+                for i in range(2)
+            ]
+            side = jnp.concatenate(halves, axis=0)
+            middle = side[256:512]
+            for t in range(3):
+                v_out[strip, t] = side[t * 256 : t * 256 + 256].astype(bf16)
+            for t in range(3):
+                v_copy(strip, t).start()
+        crossing[order] = middle
         if order == 0:
             _, line = block_place(1, strip)
 

time: 49.7 us -> 49.8 us (level)
  no operation moved by 1% of the time
where the time goes in v4:
time: 49.8 us; the launch traced here: 49.6 us
  Pallas kernels  48.3 us (97%)
  between operations  1.28 us (3%)
    pallas_call x1, Pallas kernels, on_device(): pl.pallas_call(kernel, out_shape=(pltpu.VMEM((2048, 256), bf16), pltpu.VM...  46.6 us
    pallas_call x1, Pallas kernels, on_device(): pl.pallas_call(store_results, out_shape=(jax.ShapeDtypeStruct((2048, 256)...  1.76 us

profile of v4, /device:TPU:1, one launch (start us, length us, event | category | flops | bytes accessed | tf_op | source)
XLA Modules:
  0.0 49.6 jit_solution(8793993760323181595)
XLA Ops:
  1.3 46.6 %shard_map.68 = (bf16[2048,256]{1,0:T(8,128)(2,1)S(1)}, f32[2048,256]{1,0:T(8,128)S(1)}) custom-call(s32[1]{0:T(128)S(6)} %copy.7.count_ref, bf16[256,512]{1,0:T(8,128)(2,1)} %c_hbm.1, bf16[512,512]{1,0:T(8,128)(2,1)} %bitcast.1, s32[1,512]{1,0:T(1,128)} %list_hbm.1, f32[1,512]{1,0:T(1,128)} %weight_hbm.1), custom_call_target="tpu_custom_call" | custom-call | tf_op jit(solution)/shard_map/pallas_call | solution.py:501
  47.9 1.8 %shard_map.69 = (bf16[2048,256]{1,0:T(8,128)(2,1)}, f32[2048,256]{1,0:T(8,128)}) custom-call(bf16[2048,256]{1,0:T(8,128)(2,1)S(1)} %get-tuple-element.4.density, f32[2048,256]{1,0:T(8,128)S(1)} %get-tuple-element.5.potential), custom_call_target="tpu_custom_call" | custom-call | tf_op jit(solution)/shard_map/pallas_call | solution.py:545
